TPU v7x, 256 devices: a whole 4x4x8 slice. The times are simulated.
256 devices in a mesh: row: 16 (over z, y_lo), col: 8 (over x, y_hi), rep: 2 (over core).
Axes of the slice: x: 4, y: 4 (y_hi: 2, y_lo: 2; y = y_hi * 2 + y_lo), z: 8, core: 2. Of those that a mesh axis runs over, the one named last changes fastest.
Arguments:
- activations: bfloat16 [2048, 7168], P(('col', 'rep'), 'row'), may hold values from -6 to 6
- out_grad: bfloat16 [2048, 7168], P(('col', 'rep'), 'row'), may hold values from -1.5 to 1.5
- up_codes: int32 [7168, 18432], P('row', 'col'), may hold values from 0 to 253
- up_scales: int32 [224, 18432], P('row', 'col'), may hold values from -15 to -12
- down_codes: int32 [18432, 7168], P('col', 'row'), may hold values from 0 to 253
- down_scales: int32 [576, 7168], P('col', 'row'), may hold values from -15 to -12
Outputs:
- layer_out: bfloat16 [2048, 7168], P(('col', 'rep'), 'row')
- in_grad: bfloat16 [2048, 7168], P(('col', 'rep'), 'row')
- up_grad: bfloat16 [7168, 18432], P('row', 'col')
- down_grad: bfloat16 [18432, 7168], P('col', 'row')
All inputs are finite; a program needn't handle non-finite values.
Results may differ from a plain program's by a relative error of at most 0.025.
Values may be sent and summed in bfloat16 or wider, within the bound.
A program may use at most 128 MiB of HBM per device.

v0:
```python
import jax
import jax.numpy as jnp
from jax import lax
from jax.sharding import PartitionSpec as P

BLOCK = 32


def decode(code_words, scale_exps, block_size):
    sign_bit = code_words // 127
    magnitude = code_words % 127
    exponent = magnitude // 8
    mantissa = magnitude % 8
    normal = exponent > 0
    rows_count = scale_exps.shape[0]
    cols_count = scale_exps.shape[1]
    scale_grid = jnp.broadcast_to(
        scale_exps[:, None, :], (rows_count, block_size, cols_count)
    ).reshape(code_words.shape)
    shift_count = -(jnp.where(normal, exponent - 10, -9) + scale_grid)
    factor = jnp.ones(code_words.shape, jnp.float32)
    halvings = (0.5, 0.25, 0.0625, 0.00390625, 1.52587890625e-05)
    for position in range(5):
        chosen = shift_count // 2**position % 2 == 1
        factor = factor * jnp.where(chosen, jnp.float32(halvings[position]), jnp.float32(1.0))
    mant_value = jnp.where(normal, mantissa + 8, mantissa).astype(jnp.float32)
    signed = (1 - 2 * sign_bit).astype(jnp.float32)
    return (mant_value * factor * signed).astype(jnp.bfloat16)


def gelu_parts(pre_total):
    cdf_value = 0.5 * (1.0 + jax.scipy.special.erf(pre_total * 0.7071067811865476))
    density = jnp.exp(-0.5 * pre_total * pre_total) * 0.3989422804014327
    return (pre_total * cdf_value, cdf_value + pre_total * density)


def replica_total(partial_value):
    return lax.psum(partial_value.astype(jnp.bfloat16), "rep")


def body(activations, out_grad, up_codes, up_scales, down_codes, down_scales):
    contract_last = (((1,), (1,)), ((), ()))
    contract_first = (((0,), (0,)), ((), ()))
    up_weight = decode(up_codes, up_scales, BLOCK)
    down_weight = decode(down_codes, down_scales, BLOCK)
    acts_all, grads_all = (
        lax.all_gather(activations, "col", axis=0, tiled=True),
        lax.all_gather(out_grad, "col", axis=0, tiled=True),
    )
    pre_part = jnp.dot(acts_all, up_weight, preferred_element_type=jnp.float32)
    back_part = lax.dot_general(
        grads_all, down_weight, contract_last, preferred_element_type=jnp.float32
    )
    pre_total, back_total = (
        lax.psum(pre_part.astype(jnp.bfloat16), "row").astype(jnp.float32),
        lax.psum(back_part.astype(jnp.bfloat16), "row").astype(jnp.float32),
    )
    activated, gelu_slope = gelu_parts(pre_total)
    gelu_out = activated.astype(jnp.bfloat16)
    hidden_grad = (back_total * gelu_slope).astype(jnp.bfloat16)
    down_grad = replica_total(
        lax.dot_general(gelu_out, grads_all, contract_first, preferred_element_type=jnp.float32)
    )
    out_part = jnp.dot(gelu_out, down_weight, preferred_element_type=jnp.float32)
    in_part = lax.dot_general(
        hidden_grad, up_weight, contract_last, preferred_element_type=jnp.float32
    )
    out_sum, in_sum = (
        lax.psum_scatter(
            out_part.astype(jnp.bfloat16), "col", scatter_dimension=0, tiled=True
        ).astype(jnp.float32),
        lax.psum_scatter(
            in_part.astype(jnp.bfloat16), "col", scatter_dimension=0, tiled=True
        ).astype(jnp.float32),
    )
    layer_out = out_sum.astype(jnp.bfloat16)
    in_grad = in_sum.astype(jnp.bfloat16)
    up_grad = replica_total(
        lax.dot_general(acts_all, hidden_grad, contract_first, preferred_element_type=jnp.float32)
    )
    return (layer_out, in_grad, up_grad, down_grad)


def solution(mesh):
    placed = (
        P(("col", "rep"), "row"),
        P(("col", "rep"), "row"),
        P("row", "col"),
        P("row", "col"),
        P("col", "row"),
        P("col", "row"),
    )
    return jax.shard_map(
        body,
        mesh=mesh,
        in_specs=placed,
        out_specs=(
            P(("col", "rep"), "row"),
            P(("col", "rep"), "row"),
            P("row", "col"),
            P("col", "row"),
        ),
        check_vma=False,
    )
```

profile of v0, /device:TPU:1, one launch (start us, length us, event | category | flops | bytes accessed | tf_op | source)
XLA Modules:
  0.0 786.9 jit_solution(16063781059810175605)
XLA Ops:
  7.2 0.0 all-reduce.5.cloned.1.call-start
  7.2 31.7 %all_gather.6 = bf16[1024,448]{0,1:T(8,128)(2,1)S(1)} all-gather(bf16[128,448]{0,1:T(8,128)(2,1)} %param.6), channel_id=1, replica_groups=mesh['row'=16,'col'=8,'rep'=2] {'col'}, dimensions={0}, use_global_device_ids=true | all-gather | bytes 1032192 | tf_op jit(solution)/shard_map/all_gather | solution.py:47
  38.9 28.3 %all_gather.7 = bf16[1024,448]{0,1:T(8,128)(2,1)S(1)} all-gather(bf16[128,448]{0,1:T(8,128)(2,1)} %param.7), channel_id=1, replica_groups=mesh['row'=16,'col'=8,'rep'=2] {'col'}, dimensions={0}, use_global_device_ids=true | all-gather | bytes 1032192 | tf_op jit(solution)/shard_map/all_gather | solution.py:48
  67.2 6.2 copy.14
  73.4 26.8 %fusion.42 = bf16[448,2304]{1,0:T(8,128)(2,1)S(1)} fusion(s32[448,2304]{1,0:T(8,128)} %param.8, s32[14,2304]{1,0:T(8,128)S(1)} %copy-done.7), kind=kLoop, calls=%fused_computation.127 | loop fusion | flops 155860992 | bytes 6322176 | tf_op jit(solution)/shard_map/convert_element_type | solution.py:28
  100.3 0.0 copy-start.8
  100.3 4.3 fusion.9
  104.6 29.5 %fusion.15 = bf16[2304,448]{1,0:T(8,128)(2,1)S(1)} fusion(s32[2304,448]{1,0:T(8,128)S(1)} %bitcast.27, s32[72,448]{1,0:T(8,128)S(1)} %copy-done.8), kind=kLoop, calls=%fused_computation.94 | loop fusion | flops 155860992 | bytes 6322176 | tf_op jit(solution)/shard_map/convert_element_type | solution.py:28
  134.1 4.3 fusion.10
  138.4 0.0 all-reduce.5.cloned.1.call-update
  138.4 0.0 reduce-scatter.9.cloned.1.call-start
  138.5 419.3 %all-reduce.5.cloned.1.call-done = (bf16[1024,2304]{0,1:T(8,128)(2,1)}, bf16[1024,2304]{0,1:T(8,128)(2,1)}) async-done(((bf16[1024,2304]{0,1:T(8,128)(2,1)}, bf16[1024,2304]{0,1:T(8,128)(2,1)}), (bf16[1024,2304]{0,1:T(8,128)(2,1)}, bf16[1024,2304]{0,1:T(8,128)(2,1)})) %all-reduce.5.cloned.1.call-update) | async-done | bytes 9437200 | tf_op jit(solution)/shard_map/psum | solution.py:55
  557.8 11.3 %fusion.8 = (bf16[1024,2304]{0,1:T(8,128)(2,1)S(1)}, f32[1024,2304]{0,1:T(8,128)}) fusion(bf16[1024,2304]{0,1:T(8,128)(2,1)} %get-tuple-element.4, bf16[1024,2304]{0,1:T(8,128)(2,1)} %get-tuple-element.5), kind=kLoop, calls=%fused_computation.13 | loop fusion | flops 28311552 | bytes 23592960 | tf_op jit(solution)/shard_map/convert_element_type | solution.py:60
  569.1 2.1 copy-done
  571.3 2.3 convolution_convert_fusion.4
  573.6 1.3 copy.19
  574.9 0.0 reduce-scatter.9.cloned.1.call-update
  574.9 0.2 reduce-scatter.7.cloned.1.call-start
  575.1 7.4 convolution_convert_fusion.5
  582.5 1.3 copy.17
  583.8 0.0 reduce-scatter.7.cloned.1.call-update
  583.8 0.0 all-reduce.7.cloned.1.call-start
  583.9 6.3 fusion.65
  590.2 8.7 %convolution_convert_fusion.2 = bf16[2304,448]{0,1:T(8,128)(2,1)} fusion(bf16[1024,448]{0,1:T(8,128)(2,1)S(1)} %copy-done.2, f32[1024,2304]{0,1:T(8,128)} %get-tuple-element.9, bf16[1024,2304]{0,1:T(8,128)(2,1)} %get-tuple-element.4), kind=kOutput, calls=%fused_computation.121 | convolution fusion | flops 2122039296 | bytes 17137664 | tf_op jit(solution)/shard_map/dot_general | solution.py:62
  598.9 0.0 all-reduce.7.cloned.1.call-update
  599.0 52.1 %reduce-scatter.9.cloned.1.call-done = bf16[128,448]{1,0:T(8,128)(2,1)} async-done(((bf16[1024,448]{1,0:T(8,128)(2,1)}), bf16[128,448]{1,0:T(8,128)(2,1)}) %reduce-scatter.9.cloned.1.call-update) | async-done | bytes 114704
  651.1 1.7 copy.20
  652.7 78.9 %reduce-scatter.7.cloned.1.call-done = bf16[128,448]{1,0:T(8,128)(2,1)} async-done(((bf16[1024,448]{1,0:T(8,128)(2,1)}), bf16[128,448]{1,0:T(8,128)(2,1)}) %reduce-scatter.7.cloned.1.call-update) | async-done | bytes 114704
  731.6 1.7 copy.18
  733.3 42.6 %all-reduce.7.cloned.1.call-done = (bf16[448,2304]{1,0:T(8,128)(2,1)}, bf16[2304,448]{0,1:T(8,128)(2,1)}) async-done(((bf16[448,2304]{1,0:T(8,128)(2,1)}, bf16[2304,448]{0,1:T(8,128)(2,1)}), (bf16[448,2304]{1,0:T(8,128)(2,1)}, bf16[2304,448]{0,1:T(8,128)(2,1)})) %all-reduce.7.cloned.1.call-update) | async-done | bytes 4128784 | tf_op jit(solution)/shard_map/psum | solution.py:38
  775.9 3.2 copy.25
  779.1 1.3 copy.26
  (21 shorter events, 0.0 us)
Async XLA Ops:
  7.2 550.6 %all-reduce.5.cloned.1.call-start = ((), (), s32[]{:S(2)}) async-start(), calls=%async_computation.4 | async-start | bytes 18874368 | tf_op jit(solution)/shard_map/psum | solution.py:55
  38.9 61.4 %copy-start.6 = (bf16[1024,448]{0,1:T(8,128)(2,1)}, bf16[1024,448]{0,1:T(8,128)(2,1)S(1)}, u32[]{:S(2)}) copy-start(bf16[1024,448]{0,1:T(8,128)(2,1)S(1)} %all_gather.6) | copy-start | bytes 2752516
  67.2 66.9 %copy-start.1 = (bf16[1024,448]{0,1:T(8,128)(2,1)}, bf16[1024,448]{0,1:T(8,128)(2,1)S(1)}, u32[]{:S(2)}) copy-start(bf16[1024,448]{0,1:T(8,128)(2,1)S(1)} %all_gather.7) | copy-start | bytes 2752516
  67.2 6.2 copy-start.7
  73.4 31.2 %slice-start = ((s8[4718592]{0:T(1024)(128)(4,1)}), s8[4194304]{0:T(1024)(128)(4,1)S(1)}, s32[]{:S(2)}) async-start(s8[4718592]{0:T(1024)(128)(4,1)} %bitcast.26), calls=%async_computation.6 | async-start | bytes 8388608
  100.3 4.3 copy-start.3
  100.3 4.3 slice-start.1
  100.3 4.3 copy-start.8
  138.4 512.6 %reduce-scatter.9.cloned.1.call-start = ((), (), s32[]{:S(2)}) async-start(), calls=%async_computation.3 | async-start | bytes 1179648
  557.8 13.4 %copy-start.4 = (bf16[448,2304]{1,0:T(8,128)(2,1)S(1)}, bf16[448,2304]{1,0:T(8,128)(2,1)}, u32[]{:S(2)}) copy-start(bf16[448,2304]{1,0:T(8,128)(2,1)} %copy-done.3) | copy-start | bytes 6193156
  569.1 2.1 copy-start
  574.9 156.8 %reduce-scatter.7.cloned.1.call-start = ((), (), s32[]{:S(2)}) async-start(), calls=%async_computation.2 | async-start | bytes 1179648
  583.8 6.4 copy-start.2
  583.8 192.0 %all-reduce.7.cloned.1.call-start = ((), (), s32[]{:S(2)}) async-start(), calls=%async_computation.5 | async-start | bytes 8257536 | tf_op jit(solution)/shard_map/psum | solution.py:38
  775.9 3.2 copy-start.5
Sparse Core Ops, SparseCore 0:
  138.6 419.2 all-reduce.4
  575.0 76.0 reduce-scatter.8
  655.5 76.0 reduce-scatter.6
  734.9 40.9 all-reduce.6
where the time goes:
time: 787 us
  waiting for transfers between devices  593 us (75%)
  other arithmetic  67.6 us (9%)
  blocking collectives  60 us (8%)
  matrix products  33.3 us (4%)
  local copies, waits for them, and re-layouts  18.8 us (2%)
  between operations  13.9 us (2%)
    psum x1, waiting for transfers between devices, body(): lax.psum(pre_part.astype(jnp.bfloat16), 'row').astype(jnp.float32)  419 us
    unnamed x6, waiting for transfers between devices  131 us
    convert_element_type x2, other arithmetic, decode(): return (mant_value * factor * signed).astype(jnp.bfloat16)  56.3 us
    psum x1, waiting for transfers between devices, replica_total(): return lax.psum(partial_value.astype(jnp.bfloat16), 'rep')  42.6 us
    all_gather x1, blocking collectives, body(): lax.all_gather(activations, 'col', axis=0, tiled=True)  31.7 us
    all_gather x1, blocking collectives, body(): lax.all_gather(out_grad, 'col', axis=0, tiled=True)  28.3 us
    unnamed x29, local copies, waits for them, and re-layouts  18.8 us
  transfers between devices with their start and end apart: 4, of which 4 were waited for; matrix products, arithmetic and copies ran while one was open for 3% of the time, Pallas kernels for 0%

commit v1 on v0

v1 whole, which is shorter than its diff:
```python
import functools

import jax
import jax.numpy as jnp
from jax import lax
from jax.experimental import pallas as pl
from jax.experimental.pallas import tpu as pltpu
from jax.sharding import PartitionSpec as P

MESH = pl.DeviceIdType.MESH
BLOCK = 32
NCH = 3
F32 = jnp.float32
BF16 = jnp.bfloat16
GATHER = (("ya", "yb", "xa", "xb"), ("ya", "xb", "xa", "yb"))
HALVE = (("xa", "xb", "ya", "yb"), ("yb", "ya", "xb", "xa"))


def decode(codes, scales):
    rows, cols = codes.shape
    codes = codes.reshape(rows // BLOCK, BLOCK, cols)
    negative = codes >= 127
    size = jnp.where(negative, codes - 127, codes)
    mant = (size & 7) | (jnp.minimum(size, 8) & 8)
    whole = mant << (jnp.maximum(size >> 3, 1) - 1)
    unit = (1 << (scales + 15)).astype(F32) * (2.0**-24)
    value = whole.astype(F32) * unit[:, None, :]
    return jnp.where(negative, -value, value).astype(BF16).reshape(rows, cols)


def nn(a, b):
    return jnp.dot(a, b, preferred_element_type=F32)


def nt(a, b):
    return lax.dot_general(a, b, (((1,), (1,)), ((), ())), preferred_element_type=F32)


def tn(a, b):
    return lax.dot_general(a, b, (((0,), (0,)), ((), ())), preferred_element_type=F32)


def kernel(
    nz, x_in, dy_in, wu_in, wd_in,
    lo, ig, up_out, down_out,
    tok_v, wu_v, wd_v, rs_rcv, rs_snd, pre_v, ag, ug, dg, acc, obuf, rbuf,
    gs_u, gs_d, gr_u, gr_d, nb_u, nb_d,
    loc_sem, g_snd, g_rcv, w_snd, w_rcv, rs_ss, rs_rs, ag_ss, ag_rs, p_ss, p_rs, t_snd, t_rcv, t_loc,
):
    t, feats = x_in.shape[1], x_in.shape[2]
    hid = wu_in.shape[1] // 2
    ch = hid // NCH
    fh, chh = feats // 2, ch // 2
    row, col, rep = lax.axis_index("row"), lax.axis_index("col"), lax.axis_index("rep")
    z, yl = row // 2, row % 2
    xx, yh = col // 2, col % 2
    oh, orep = 1 - yl, 1 - rep

    def place(dims):
        a, b = int("ya" in dims), int("yb" in dims)
        nyl, nyh = (yl + a + b) % 2, (yh + b) % 2
        if "xa" in dims and "xb" in dims:
            nx = (xx + 2) % 4
        elif "xa" in dims:
            nx = xx + 1 - 2 * (xx % 2)
        elif "xb" in dims:
            nx = 3 - xx
        else:
            nx = xx
        return nyl, 2 * nx + nyh

    def plane(dim):
        nyl, ncol = place((dim,))
        return (2 * z + nyl, ncol, rep)

    zp = (2 * ((z + 1) % nz) + yl, col, rep)
    zm = (2 * ((z + nz - 1) % nz) + yl, col, rep)
    twin = (row, col, orep)
    ring = (zp, zm)

    def remote(src, dst, ssem, rsem, dev):
        return pltpu.make_async_remote_copy(
            src_ref=src, dst_ref=dst, send_sem=ssem, recv_sem=rsem, device_id=dev, device_id_type=MESH
        )

    barrier = pltpu.get_barrier_semaphore()
    for dev in (zp, zm, twin, plane("ya"), plane("yb"), plane("xa"), plane("xb")):
        pl.semaphore_signal(barrier, inc=1, device_id=dev, device_id_type=MESH)
    pl.semaphore_wait(barrier, 7)

    def lanes(half, j):
        return pl.ds(pl.multiple_of(half * hid + j * ch, 128), ch)

    def rows(start, size):
        return pl.ds(pl.multiple_of(start, 16), size)

    def w_first(m, j):
        if m == 0:
            src = wu_in.at[rows(rep * fh, fh), lanes(oh, j)]
            dst = wu_v.at[j, yl, rows(rep * fh, fh)]
        else:
            src = wd_in.at[rows(oh * hid + j * ch + rep * chh, chh)]
            dst = wd_v.at[j, yl, rows(rep * chh, chh)]
        return remote(src, dst, w_snd.at[0, m, j], w_rcv.at[0, m, j], plane("ya"))

    def w_second(m, j):
        ref = (wu_v.at[j, oh, rows(rep * fh, fh)], wd_v.at[j, oh, rows(rep * chh, chh)])[m]
        return remote(ref, ref, w_snd.at[1, m, j], w_rcv.at[1, m, j], twin)

    def w_local(m, j):
        if m == 0:
            return pltpu.make_async_copy(wu_in.at[:, lanes(yl, j)], wu_v.at[j, yl], loc_sem.at[m, j])
        return pltpu.make_async_copy(wd_in.at[rows(yl * hid + j * ch, ch)], wd_v.at[j, yl], loc_sem.at[m, j])

    tok_in = (x_in, dy_in)

    def spot(m, code):
        dims = tuple(GATHER[m][k] for k in range(4) if code >> k & 1)
        nyl, ncol = place(dims)
        return tok_v.at[m, nyl, :, rows(ncol * t, t)]

    def g_copy(m, code, step):
        src = tok_in[m] if code == 0 else spot(m, code)
        new = code + 2**step
        return remote(src, spot(m, code), g_snd.at[m, new], g_rcv.at[m, new], plane(GATHER[m][step]))

    def g_wait(m, code):
        here = spot(m, code)
        remote(here, here, g_snd.at[m, code], g_rcv.at[m, code], twin).wait_recv()

    for step in range(1, 4):
        for m in range(2):
            g_copy(m, 0, step).start()
    for m in range(2):
        g_copy(m, 0, 0).start()
    for j in range(NCH):
        for m in range(2):
            w_first(m, j).start()
    tok_local = [pltpu.make_async_copy(tok_in[m], spot(m, 0), loc_sem.at[2, m]) for m in range(2)]
    for m in range(2):
        tok_local[m].start()
        for j in range(NCH):
            w_local(m, j).start()

    ug[...] = jnp.zeros_like(ug)
    dg[...] = jnp.zeros_like(dg)
    for m in range(2):
        for j in range(NCH):
            rs_rcv[m, j, 0] = jnp.zeros(rs_rcv.shape[3:], BF16)

    for code in range(1, 16):
        for m in range(2):
            g_wait(m, code)
            for step in range(4):
                if 2**step > code:
                    g_copy(m, code, step).start()
    for m in range(2):
        tok_local[m].wait()

    def rs_copy(m, j, s):
        return remote(rs_snd.at[m, j, s], rs_rcv.at[m, j, s + 1], rs_ss.at[m, j, s], rs_rs.at[m, j, s + 1], ring[m])

    def rs_wait(m, j, s):
        here = rs_rcv.at[m, j, s]
        remote(here, here, rs_ss.at[m, j, s], rs_rs.at[m, j, s], twin).wait_recv()

    def term(m, j, b):
        if m == 0:
            return nn(tok_v[0, 0, b], wu_v[j, 0]) + nn(tok_v[0, 1, b], wu_v[j, 1])
        return nt(tok_v[1, 0, b], wd_v[j, 0]) + nt(tok_v[1, 1, b], wd_v[j, 1])

    def rs_step(i, carry):
        s, j = i // NCH, i % NCH

        @pl.when(s == 0)
        def _():
            for m in range(2):
                w_first(m, j).wait_recv()
                w_second(m, j).start()
            for m in range(2):
                w_local(m, j).wait()
                w_second(m, j).wait_recv()

        for m in range(2):
            b = (z + nz - 1 - s) % nz if m == 0 else (z + 1 + s) % nz
            part = term(m, j, b)

            @pl.when(s > 0)
            def _():
                rs_wait(m, j, s)

            rs_snd[m, j, s] = (part + rs_rcv[m, j, s].astype(F32)).astype(BF16)
            rs_copy(m, j, s).start()
        return carry

    lax.fori_loop(0, NCH * (nz - 1), rs_step, 0)

    def ag_copy(m, j, s):
        return remote(ag.at[m, j, s], ag.at[m, j, s + 1], ag_ss.at[m, j, s], ag_rs.at[m, j, s + 1], ring[m])

    def ag_wait(m, j, s):
        here = ag.at[m, j, s]
        remote(here, here, ag_ss.at[m, j, s], ag_rs.at[m, j, s], twin).wait_recv()

    def gelu_step(j, carry):
        for m in range(2):
            pre_v[m] = term(m, j, z)
        for m in range(2):
            rs_wait(m, j, nz - 1)
        pre = pre_v[0] + rs_rcv[0, j, nz - 1].astype(F32)
        back = pre_v[1] + rs_rcv[1, j, nz - 1].astype(F32)
        cdf = 0.5 * (1.0 + lax.erf(pre * 0.7071067811865476))
        density = jnp.exp(-0.5 * pre * pre) * 0.3989422804014327
        ag[0, j, 0] = (pre * cdf).astype(BF16)
        ag[1, j, 0] = (back * (cdf + pre * density)).astype(BF16)
        for m in range(2):
            ag_copy(m, j, 0).start()
        return carry

    lax.fori_loop(0, NCH, gelu_step, 0)

    widths = (8, 4, 2, 1)
    offs = (0, 8, 12, 14)

    def p_copy(m, k, s):
        w = widths[k]
        return remote(
            obuf.at[m, s, pl.ds(w, w)], rbuf.at[m, s, pl.ds(offs[k], w)],
            p_ss.at[m, k, s], p_rs.at[m, k, s], plane(HALVE[m][k]),
        )

    def p_first(m, s):
        for code in range(16):
            dims = tuple(HALVE[m][k] for k in range(4) if code >> (3 - k) & 1)
            nyl, ncol = place(dims)
            obuf[m, s, code] = acc[m, nyl, rows(ncol * t, t)].astype(BF16)
        p_copy(m, 0, s).start()

    def p_next(m, k, s):
        w = widths[k]
        p_copy(m, k, s).wait_recv()
        both = obuf[m, s, 0:w].astype(F32) + rbuf[m, s, offs[k] : offs[k] + w].astype(F32)
        if k < 3:
            obuf[m, s, 0:w] = both.astype(BF16)
            p_copy(m, k + 1, s).start()
        else:
            b = (z + nz - s) % nz if m == 0 else (z + s) % nz
            (lo, ig)[m][rows(b * t, t)] = both[0].astype(BF16)

    def p_step(s):
        for k in range(3, -1, -1):
            q = s - 1 - k

            @pl.when(jnp.logical_and(q >= 0, q < nz))
            def _():
                for m in range(2):
                    p_next(m, k, q)

    def ag_step(i, carry):
        s, j = i // NCH, i % NCH
        for m in range(2):

            @pl.when(s > 0)
            def _():
                ag_wait(m, j, s)

            @pl.when(jnp.logical_and(s > 0, s < nz - 1))
            def _():
                ag_copy(m, j, s).start()

        @pl.when(j == 0)
        def _():
            acc[...] = jnp.zeros_like(acc)

        for y in range(2):
            acc[0, y] += nn(ag[0, j, s], wd_v[j, y])
            acc[1, y] += nt(ag[1, j, s], wu_v[j, y])

        @pl.when(s % 2 == 1)
        def _():
            a_pair = jnp.concatenate([ag[0, j, s - 1], ag[0, j, s]], axis=0)
            h_pair = jnp.concatenate([ag[1, j, s - 1], ag[1, j, s]], axis=0)
            a0, a1 = (z + nz - s + 1) % nz, (z + nz - s) % nz
            h0, h1 = (z + s - 1) % nz, (z + s) % nz
            for y in range(2):
                dg[j, y] += tn(a_pair, jnp.concatenate([tok_v[1, y, a0], tok_v[1, y, a1]], axis=0))
                ug[j, y] += tn(jnp.concatenate([tok_v[0, y, h0], tok_v[0, y, h1]], axis=0), h_pair)

        @pl.when(j == NCH - 1)
        def _():
            for m in range(2):
                p_first(m, s)
            p_step(s)

        return carry

    lax.fori_loop(0, NCH * nz, ag_step, 0)

    def t_pair(m, j):
        src, dst = ((gs_u, gr_u), (gs_d, gr_d))[m]
        return remote(src.at[j], dst.at[j], t_snd.at[0, m, j], t_rcv.at[0, m, j], twin)

    def grad_half(m, j, y, who):
        if m == 0:
            return ug[j, y, rows(who * fh, fh)]
        return dg[j, y, rows(who * chh, chh)]

    def home(m, j, half, who):
        if m == 0:
            return up_out.at[rows(who * fh, fh), lanes(half, j)]
        return down_out.at[rows(half * hid + j * ch + who * chh, chh)]

    mine = (gr_u, gr_d)
    near = (nb_u, nb_d)

    def t_near(m, j):
        return remote(mine[m].at[j, oh], near[m].at[j], t_snd.at[1, m, j], t_rcv.at[1, m, j], plane("ya"))

    def t_own(m, j):
        return pltpu.make_async_copy(mine[m].at[j, yl], home(m, j, yl, rep), t_loc.at[0, m, j])

    def t_twin(m, j, who):
        return remote(mine[m].at[j, yl], home(m, j, yl, who), t_snd.at[2, m, j], t_rcv.at[2, m, j], twin)

    def t_far(m, j):
        return pltpu.make_async_copy(near[m].at[j], home(m, j, oh, rep), t_loc.at[1, m, j])

    def t_relay(m, j, who):
        return remote(near[m].at[j], home(m, j, oh, who), t_snd.at[3, m, j], t_rcv.at[3, m, j], twin)

    def t_a(j, carry):
        for m in range(2):
            for y in range(2):
                (gs_u, gs_d)[m][j, y] = grad_half(m, j, y, orep).astype(BF16)
            t_pair(m, j).start()
        return carry

    lax.fori_loop(0, NCH, t_a, 0)
    p_step(nz)

    def t_b(j, carry):
        for m in range(2):
            t_pair(m, j).wait_recv()
            for y in range(2):
                mine[m][j, y] = (grad_half(m, j, y, rep) + mine[m][j, y].astype(F32)).astype(BF16)
            t_near(m, j).start()
            t_own(m, j).start()
            t_twin(m, j, rep).start()
        return carry

    lax.fori_loop(0, NCH, t_b, 0)
    for s in range(nz + 1, nz + 4):
        p_step(s)

    def t_c(j, carry):
        for m in range(2):
            t_near(m, j).wait_recv()
            t_far(m, j).start()
            t_relay(m, j, rep).start()
        return carry

    lax.fori_loop(0, NCH, t_c, 0)

    def drain_t(j, carry):
        for m in range(2):
            t_own(m, j).wait()
            t_far(m, j).wait()
            t_twin(m, j, orep).wait_recv()
            t_relay(m, j, orep).wait_recv()
            t_pair(m, j).wait_send()
            t_near(m, j).wait_send()
            t_twin(m, j, rep).wait_send()
            t_relay(m, j, rep).wait_send()
            w_first(m, j).wait_send()
            w_second(m, j).wait_send()
        return carry

    lax.fori_loop(0, NCH, drain_t, 0)

    def drain_ring(i, carry):
        s, j = i // NCH, i % NCH
        for m in range(2):
            rs_copy(m, j, s).wait_send()
            ag_copy(m, j, s).wait_send()
        return carry

    lax.fori_loop(0, NCH * (nz - 1), drain_ring, 0)

    def drain_plane(s, carry):
        for m in range(2):
            for k in range(4):
                p_copy(m, k, s).wait_send()
        return carry

    lax.fori_loop(0, nz, drain_plane, 0)
    for m in range(2):
        for code in range(8):
            for step in range(4):
                if 2**step > code:
                    g_copy(m, code, step).wait_send()


def body(n_row, n_col, activations, out_grad, up_codes, up_scales, down_codes, down_scales):
    nz = n_row // 2
    tok, feats = activations.shape
    t = tok // nz
    hid2 = up_codes.shape[1]
    hid = hid2 // 2
    ch = hid // NCH
    span = n_col * t
    wu = decode(up_codes, up_scales)
    wd = decode(down_codes, down_scales)
    x = activations.reshape(nz, t, feats)
    dy = out_grad.reshape(nz, t, feats)
    hbm = pl.BlockSpec(memory_space=pl.ANY)
    vmem = pl.BlockSpec(memory_space=pltpu.VMEM)
    dma = pltpu.SemaphoreType.DMA
    return pl.pallas_call(
        functools.partial(kernel, nz),
        out_shape=(
            jax.ShapeDtypeStruct((tok, feats), BF16),
            jax.ShapeDtypeStruct((tok, feats), BF16),
            jax.ShapeDtypeStruct((feats, hid2), BF16),
            jax.ShapeDtypeStruct((hid2, feats), BF16),
        ),
        in_specs=[hbm] * 4,
        out_specs=(vmem, vmem, hbm, hbm),
        scratch_shapes=[
            pltpu.VMEM((2, 2, nz, span, feats), BF16),
            pltpu.VMEM((NCH, 2, feats, ch), BF16),
            pltpu.VMEM((NCH, 2, ch, feats), BF16),
            pltpu.VMEM((2, NCH, nz, span, ch), BF16),
            pltpu.VMEM((2, NCH, nz - 1, span, ch), BF16),
            pltpu.VMEM((2, span, ch), F32),
            pltpu.VMEM((2, NCH, nz, span, ch), BF16),
            pltpu.VMEM((NCH, 2, feats, ch), F32),
            pltpu.VMEM((NCH, 2, ch, feats), F32),
            pltpu.VMEM((2, 2, span, feats), F32),
            pltpu.VMEM((2, nz, 16, t, feats), BF16),
            pltpu.VMEM((2, nz, 15, t, feats), BF16),
            pltpu.VMEM((NCH, 2, feats // 2, ch), BF16),
            pltpu.VMEM((NCH, 2, ch // 2, feats), BF16),
            pltpu.VMEM((NCH, 2, feats // 2, ch), BF16),
            pltpu.VMEM((NCH, 2, ch // 2, feats), BF16),
            pltpu.VMEM((NCH, feats // 2, ch), BF16),
            pltpu.VMEM((NCH, ch // 2, feats), BF16),
            dma((3, NCH)),
            dma((2, 16)),
            dma((2, 16)),
            dma((2, 2, NCH)),
            dma((2, 2, NCH)),
            dma((2, NCH, nz)),
            dma((2, NCH, nz)),
            dma((2, NCH, nz)),
            dma((2, NCH, nz)),
            dma((2, 4, nz)),
            dma((2, 4, nz)),
            dma((4, 2, NCH)),
            dma((4, 2, NCH)),
            dma((2, 2, NCH)),
        ],
        compiler_params=pltpu.CompilerParams(
            collective_id=0, has_side_effects=True, vmem_limit_bytes=62 * 1024 * 1024
        ),
        name="ffn_ring",
    )(x, dy, wu, wd)


def solution(mesh):
    tokens = P(("col", "rep"), "row")
    up, down = P("row", "col"), P("col", "row")
    return jax.shard_map(
        functools.partial(body, mesh.shape["row"], mesh.shape["col"]),
        mesh=mesh,
        in_specs=(tokens, tokens, up, up, down, down),
        out_specs=(tokens, tokens, up, down),
        check_vma=False,
    )
```

time: 787 us -> 203 us (0.26)
  waiting for transfers between devices: 593 us -> 0 us
  Pallas kernels: 0 us -> 178 us
  blocking collectives: 60 us -> 0 us
  other arithmetic: 67.6 us -> 8.93 us
  matrix products: 33.3 us -> 0 us
  between operations: 13.9 us -> 0.71 us
    psum x2 -> x0, waiting for transfers between devices: 462 us -> none  [the longest x1 419 us: body(): lax.psum(pre_part.astype(jnp.bfloat16), 'row').astype(jnp.float32)]
    pallas_call x0 -> x1, Pallas kernels: none -> 178 us  [body(): pl.pallas_call(functools.partial(kernel, nz), out_shape=(jax.ShapeDtypeSt...]
    unnamed x6 -> x0, waiting for transfers between devices: 131 us -> none
    all_gather x2 -> x0, blocking collectives: 60 us -> none  [the longest x1 31.7 us: body(): lax.all_gather(activations, 'col', axis=0, tiled=True)]
    convert_element_type x3 -> x2, other arithmetic: 67.6 us -> 8.88 us  [decode(): return jnp.where(negative, -value, value).astype(BF16).reshape(rows, cols)]
    dot_general x6 -> x0, matrix products: 33.3 us -> none  [the longest x1 8.72 us: body(): lax.dot_general(gelu_out, grads_all, contract_first, preferred_element_ty...]
    unnamed x29 -> x20, local copies, waits for them, and re-layouts: 18.8 us -> 8.72 us
  transfers between devices with their start and end apart: 4 -> 0, of which waited for: 4 -> 0; matrix products, arithmetic and copies ran while one was open for 3% -> 0% of each run, Pallas kernels for 0% -> 0%
where the time goes in v1:
time: 203 us; the launch traced here: 202 us
  Pallas kernels  178 us (88%)
  local copies, waits for them, and re-layouts  14.5 us (7%)
  other arithmetic  8.93 us (4%)
    pallas_call x1, Pallas kernels, body(): pl.pallas_call(functools.partial(kernel, nz), out_shape=(jax.ShapeDtypeSt...  178 us
    convert_element_type x2, other arithmetic, decode(): return jnp.where(negative, -value, value).astype(BF16).reshape(rows, cols)  8.88 us
    unnamed x20, local copies, waits for them, and re-layouts  8.72 us
    pallas_call x3, local copies, waits for them, and re-layouts, body(): pl.pallas_call(functools.partial(kernel, nz), out_shape=(jax.ShapeDtypeSt...  5.82 us

profile of v1, /device:TPU:1, one launch (start us, length us, event | category | flops | bytes accessed | tf_op | source)
XLA Modules:
  0.0 202.3 jit_solution(12028017060191781941)
XLA Ops:
  0.6 0.0 copy-start.2
  0.6 5.8 %copy.12 = s32[2304,448]{1,0:T(8,128)} copy(s32[2304,448]{0,1:T(8,128)} %param.10) | data formatting | bytes 8257536 | tf_op args[4]
  6.5 0.0 copy-done.2
  6.5 0.0 copy-start.3
  6.5 0.0 copy-start
  6.5 5.5 %fusion.wd_in = bf16[2304,448]{1,0:T(8,128)(2,1)} fusion(s32[2304,448]{1,0:T(8,128)} %copy.12, f32[72,448]{1,0:T(8,128)S(1)} %convert_multiply_fusion), kind=kLoop, calls=%fused_computation.4 | loop fusion | flops 16515072 | bytes 6322176 | tf_op jit(solution)/shard_map/convert_element_type | solution.py:28
  12.1 0.0 copy-done.3
  12.1 0.0 copy-start.6
  12.1 0.0 copy-start.7
  12.1 0.0 copy-done
  12.1 3.3 %fusion.2.wu_in = bf16[448,2304]{1,0:T(8,128)(2,1)} fusion(s32[448,2304]{1,0:T(8,128)S(1)} %copy-done, f32[14,2304]{1,0:T(8,128)S(1)} %convert_multiply_fusion.1), kind=kLoop, calls=%fused_computation.7 | loop fusion | flops 16515072 | bytes 6322176 | tf_op jit(solution)/shard_map/convert_element_type | solution.py:28
  15.5 0.0 copy-done.6
  15.5 0.8 copy.10
  16.2 0.0 copy-done.7
  16.2 0.8 copy.11
  17.0 178.1 %ffn_ring.1 = (bf16[128,448]{1,0:T(8,128)(2,1)}, bf16[128,448]{1,0:T(8,128)(2,1)}, bf16[448,2304]{1,0:T(8,128)(2,1)}, bf16[2304,448]{1,0:T(8,128)(2,1)}) custom-call(bf16[8,16,448]{2,1,0:T(8,128)(2,1)} %bitcast.10, bf16[8,16,448]{2,1,0:T(8,128)(2,1)} %bitcast.11, bf16[448,2304]{1,0:T(8,128)(2,1)} %fusion.2.wu_in, bf16[2304,448]{1,0:T(8,128)(2,1)} %fusion.wd_in), custom_call_target="tpu_custom_call" | custom-call | tf_op jit(solution)/shard_map/ffn_ring/pallas_call | solution.py:418
  195.2 0.0 copy-start.5
  195.2 0.0 copy-start.4
  195.2 0.0 copy-start.1
  195.2 4.3 %copy.17 = bf16[2304,448]{0,1:T(8,128)(2,1)} copy(bf16[2304,448]{1,0:T(8,128)(2,1)} %get-tuple-element.7) | data formatting | bytes 4128768 | tf_op jit(solution)/shard_map/ffn_ring/pallas_call | solution.py:418
  199.5 0.0 copy-done.5
  199.5 0.8 copy.15
  200.2 0.0 copy-done.4
  200.2 0.8 copy.16
  201.0 0.0 copy-done.1
  201.0 1.3 copy.19
  (2 shorter events, 0.0 us)
Async XLA Ops:
  0.6 5.9 %copy-start.2 = (s32[72,448]{1,0:T(8,128)S(1)}, s32[72,448]{1,0:T(8,128)}, u32[]{:S(2)}) copy-start(s32[72,448]{1,0:T(8,128)} %param.11) | copy-start | bytes 387076
  6.5 5.6 %copy-start.3 = (s32[14,2304]{1,0:T(8,128)S(1)}, s32[14,2304]{1,0:T(8,128)}, u32[]{:S(2)}) copy-start(s32[14,2304]{1,0:T(8,128)} %param.9) | copy-start | bytes 387076
  6.5 5.6 %copy-start = (s32[448,2304]{1,0:T(8,128)S(1)}, s32[448,2304]{1,0:T(8,128)}, u32[]{:S(2)}) copy-start(s32[448,2304]{1,0:T(8,128)} %param.8) | copy-start | bytes 12386308
  12.1 3.4 %copy-start.6 = (bf16[128,448]{0,1:T(8,128)(2,1)S(1)}, bf16[128,448]{0,1:T(8,128)(2,1)}, u32[]{:S(2)}) copy-start(bf16[128,448]{0,1:T(8,128)(2,1)} %param.6) | copy-start | bytes 344068
  12.1 4.2 %copy-start.7 = (bf16[128,448]{0,1:T(8,128)(2,1)S(1)}, bf16[128,448]{0,1:T(8,128)(2,1)}, u32[]{:S(2)}) copy-start(bf16[128,448]{0,1:T(8,128)(2,1)} %param.7) | copy-start | bytes 344068
  195.2 4.3 %copy-start.5 = (bf16[128,448]{1,0:T(8,128)(2,1)S(1)}, bf16[128,448]{1,0:T(8,128)(2,1)}, u32[]{:S(2)}) copy-start(bf16[128,448]{1,0:T(8,128)(2,1)} %get-tuple-element.4) | copy-start | bytes 344068
  195.2 5.1 %copy-start.4 = (bf16[128,448]{1,0:T(8,128)(2,1)S(1)}, bf16[128,448]{1,0:T(8,128)(2,1)}, u32[]{:S(2)}) copy-start(bf16[128,448]{1,0:T(8,128)(2,1)} %get-tuple-element.5) | copy-start | bytes 344068
  195.2 5.8 %copy-start.1 = (bf16[448,2304]{1,0:T(8,128)(2,1)S(1)}, bf16[448,2304]{1,0:T(8,128)(2,1)}, u32[]{:S(2)}) copy-start(bf16[448,2304]{1,0:T(8,128)(2,1)} %get-tuple-element.14) | copy-start | bytes 6193156

commit v2 on v1

--- a/solution.py
+++ b/solution.py
@@ -16,16 +16,17 @@
 HALVE = (("xa", "xb", "ya", "yb"), ("yb", "ya", "xb", "xa"))
 
 
-def decode(codes, scales):
-    rows, cols = codes.shape
-    codes = codes.reshape(rows // BLOCK, BLOCK, cols)
+def decode(codes, unit):
     negative = codes >= 127
     size = jnp.where(negative, codes - 127, codes)
     mant = (size & 7) | (jnp.minimum(size, 8) & 8)
-    whole = mant << (jnp.maximum(size >> 3, 1) - 1)
-    unit = (1 << (scales + 15)).astype(F32) * (2.0**-24)
-    value = whole.astype(F32) * unit[:, None, :]
-    return jnp.where(negative, -value, value).astype(BF16).reshape(rows, cols)
+    whole = jnp.left_shift(mant, jnp.maximum(jnp.right_shift(size, 3), 1) - 1)
+    value = whole.astype(F32) * unit
+    return jnp.where(negative, -value, value).astype(BF16)
+
+
+def units(scales):
+    return jnp.left_shift(jnp.ones_like(scales), scales + 15).astype(F32) * (2.0**-24)
 
 
 def nn(a, b):
@@ -41,16 +42,16 @@
 
 
 def kernel(
-    nz, x_in, dy_in, wu_in, wd_in,
+    nz, x_in, dy_in, cu_in, cd_in, su_in, sd_in,
     lo, ig, up_out, down_out,
     tok_v, wu_v, wd_v, rs_rcv, rs_snd, pre_v, ag, ug, dg, acc, obuf, rbuf,
-    gs_u, gs_d, gr_u, gr_d, nb_u, nb_d,
-    loc_sem, g_snd, g_rcv, w_snd, w_rcv, rs_ss, rs_rs, ag_ss, ag_rs, p_ss, p_rs, t_snd, t_rcv, t_loc,
+    gs_u, gs_d, gr_u, gr_d, nb_u, nb_d, c_own, c_far, w_snd_v, unit_v,
+    loc_sem, c_sem, g_snd, g_rcv, w_snd, w_rcv, rs_ss, rs_rs, ag_ss, ag_rs, p_ss, p_rs, t_snd, t_rcv, t_loc,
 ):
     t, feats = x_in.shape[1], x_in.shape[2]
-    hid = wu_in.shape[1] // 2
+    hid = cu_in.shape[1] // 2
     ch = hid // NCH
-    fh, chh = feats // 2, ch // 2
+    fh = feats // 2
     row, col, rep = lax.axis_index("row"), lax.axis_index("col"), lax.axis_index("rep")
     z, yl = row // 2, row % 2
     xx, yh = col // 2, col % 2
@@ -83,34 +84,61 @@
             src_ref=src, dst_ref=dst, send_sem=ssem, recv_sem=rsem, device_id=dev, device_id_type=MESH
         )
 
+    def lanes(half, j):
+        return pl.ds(pl.multiple_of(half * hid + j * ch, 128), ch)
+
+    def rows(start, size):
+        return pl.ds(pl.multiple_of(start, 16), size)
+
+    def code_copy(m, j, far):
+        src = (cu_in, cd_in)[m]
+        if far:
+            return pltpu.make_async_copy(src.at[rows(rep * fh, fh), lanes(oh, j)], c_far.at[m, j], c_sem.at[1, m, j])
+        return pltpu.make_async_copy(src.at[:, lanes(yl, j)], c_own.at[m, j], c_sem.at[0, m, j])
+
+    for far in (True, False):
+        for j in range(NCH):
+            for m in range(2):
+                code_copy(m, j, far).start()
+
     barrier = pltpu.get_barrier_semaphore()
     for dev in (zp, zm, twin, plane("ya"), plane("yb"), plane("xa"), plane("xb")):
         pl.semaphore_signal(barrier, inc=1, device_id=dev, device_id_type=MESH)
     pl.semaphore_wait(barrier, 7)
 
-    def lanes(half, j):
-        return pl.ds(pl.multiple_of(half * hid + j * ch, 128), ch)
-
-    def rows(start, size):
-        return pl.ds(pl.multiple_of(start, 16), size)
-
     def w_first(m, j):
-        if m == 0:
-            src = wu_in.at[rows(rep * fh, fh), lanes(oh, j)]
-            dst = wu_v.at[j, yl, rows(rep * fh, fh)]
-        else:
-            src = wd_in.at[rows(oh * hid + j * ch + rep * chh, chh)]
-            dst = wd_v.at[j, yl, rows(rep * chh, chh)]
-        return remote(src, dst, w_snd.at[0, m, j], w_rcv.at[0, m, j], plane("ya"))
+        dst = (wu_v, wd_v)[m].at[j, yl, rows(rep * fh, fh)]
+        return remote(w_snd_v.at[m, j], dst, w_snd.at[0, m, j], w_rcv.at[0, m, j], plane("ya"))
 
     def w_second(m, j):
-        ref = (wu_v.at[j, oh, rows(rep * fh, fh)], wd_v.at[j, oh, rows(rep * chh, chh)])[m]
+        ref = (wu_v, wd_v)[m].at[j, oh, rows(rep * fh, fh)]
         return remote(ref, ref, w_snd.at[1, m, j], w_rcv.at[1, m, j], twin)
 
-    def w_local(m, j):
-        if m == 0:
-            return pltpu.make_async_copy(wu_in.at[:, lanes(yl, j)], wu_v.at[j, yl], loc_sem.at[m, j])
-        return pltpu.make_async_copy(wd_in.at[rows(yl * hid + j * ch, ch)], wd_v.at[j, yl], loc_sem.at[m, j])
+    def w_decode(m, j, far):
+        code_copy(m, j, far).wait()
+        count = (fh if far else feats) // BLOCK
+        base = rep * (fh // BLOCK) if far else 0
+        half = oh if far else yl
+        if m == 1:
+            groups = sd_in.shape[0]
+            lane = lax.broadcasted_iota(jnp.int32, (groups, ch), 1) + half * hid + j * ch
+            group = lax.broadcasted_iota(jnp.int32, (groups, ch), 0)
+            pick = jnp.where(jnp.right_shift(lane, 5) == group, 1.0, 0.0)
+            unit_v[...] = tn(units(sd_in[...]), pick)
+
+        def step(b, carry):
+            here = rows(b * BLOCK, BLOCK)
+            if m == 0:
+                unit = units(su_in[pl.ds(base + b, 1), lanes(half, j)])
+            else:
+                unit = unit_v[rows((base + b) * BLOCK, BLOCK)]
+            if far:
+                w_snd_v[m, j, here] = decode(c_far[m, j, here], unit)
+            else:
+                (wu_v, wd_v)[m][j, yl, here] = decode(c_own[m, j, here], unit)
+            return carry
+
+        lax.fori_loop(0, count, step, 0)
 
     tok_in = (x_in, dy_in)
 
@@ -133,22 +161,44 @@
             g_copy(m, 0, step).start()
     for m in range(2):
         g_copy(m, 0, 0).start()
-    for j in range(NCH):
-        for m in range(2):
-            w_first(m, j).start()
     tok_local = [pltpu.make_async_copy(tok_in[m], spot(m, 0), loc_sem.at[2, m]) for m in range(2)]
     for m in range(2):
         tok_local[m].start()
-        for j in range(NCH):
-            w_local(m, j).start()
-
-    ug[...] = jnp.zeros_like(ug)
-    dg[...] = jnp.zeros_like(dg)
-    for m in range(2):
-        for j in range(NCH):
-            rs_rcv[m, j, 0] = jnp.zeros(rs_rcv.shape[3:], BF16)
-
+
+    def w_send(j):
+        for m in range(2):
+            w_decode(m, j, True)
+            w_first(m, j).start()
+
+    def w_relay(j):
+        for m in range(2):
+            w_first(m, j).wait_recv()
+            w_second(m, j).start()
+
+    def clear():
+        ug[...] = jnp.zeros_like(ug)
+        dg[...] = jnp.zeros_like(dg)
+        for m in range(2):
+            for j in range(NCH):
+                rs_rcv[m, j, 0] = jnp.zeros(rs_rcv.shape[3:], BF16)
+
+    between = {
+        2: lambda: w_send(1),
+        3: lambda: w_send(2),
+        4: lambda: w_decode(0, 0, False),
+        5: lambda: w_decode(1, 0, False),
+        6: lambda: w_decode(0, 1, False),
+        7: lambda: w_decode(1, 1, False),
+        8: lambda: w_decode(0, 2, False),
+        9: lambda: w_decode(1, 2, False),
+        10: clear,
+        12: lambda: w_relay(0),
+        14: lambda: w_relay(1),
+    }
+    w_send(0)
     for code in range(1, 16):
+        if code in between:
+            between[code]()
         for m in range(2):
             g_wait(m, code)
             for step in range(4):
@@ -167,18 +217,18 @@
     def term(m, j, b):
         if m == 0:
             return nn(tok_v[0, 0, b], wu_v[j, 0]) + nn(tok_v[0, 1, b], wu_v[j, 1])
-        return nt(tok_v[1, 0, b], wd_v[j, 0]) + nt(tok_v[1, 1, b], wd_v[j, 1])
+        return nn(tok_v[1, 0, b], wd_v[j, 0]) + nn(tok_v[1, 1, b], wd_v[j, 1])
 
     def rs_step(i, carry):
         s, j = i // NCH, i % NCH
+
+        @pl.when(i == 1)
+        def _():
+            w_relay(2)
 
         @pl.when(s == 0)
         def _():
             for m in range(2):
-                w_first(m, j).wait_recv()
-                w_second(m, j).start()
-            for m in range(2):
-                w_local(m, j).wait()
                 w_second(m, j).wait_recv()
 
         for m in range(2):
@@ -273,7 +323,7 @@
             acc[...] = jnp.zeros_like(acc)
 
         for y in range(2):
-            acc[0, y] += nn(ag[0, j, s], wd_v[j, y])
+            acc[0, y] += nt(ag[0, j, s], wd_v[j, y])
             acc[1, y] += nt(ag[1, j, s], wu_v[j, y])
 
         @pl.when(s % 2 == 1)
@@ -283,7 +333,7 @@
             a0, a1 = (z + nz - s + 1) % nz, (z + nz - s) % nz
             h0, h1 = (z + s - 1) % nz, (z + s) % nz
             for y in range(2):
-                dg[j, y] += tn(a_pair, jnp.concatenate([tok_v[1, y, a0], tok_v[1, y, a1]], axis=0))
+                dg[j, y] += tn(jnp.concatenate([tok_v[1, y, a0], tok_v[1, y, a1]], axis=0), a_pair)
                 ug[j, y] += tn(jnp.concatenate([tok_v[0, y, h0], tok_v[0, y, h1]], axis=0), h_pair)
 
         @pl.when(j == NCH - 1)
@@ -301,14 +351,10 @@
         return remote(src.at[j], dst.at[j], t_snd.at[0, m, j], t_rcv.at[0, m, j], twin)
 
     def grad_half(m, j, y, who):
-        if m == 0:
-            return ug[j, y, rows(who * fh, fh)]
-        return dg[j, y, rows(who * chh, chh)]
+        return (ug, dg)[m][j, y, rows(who * fh, fh)]
 
     def home(m, j, half, who):
-        if m == 0:
-            return up_out.at[rows(who * fh, fh), lanes(half, j)]
-        return down_out.at[rows(half * hid + j * ch + who * chh, chh)]
+        return (up_out, down_out)[m].at[rows(who * fh, fh), lanes(half, j)]
 
     mine = (gr_u, gr_d)
     near = (nb_u, nb_d)
@@ -408,43 +454,46 @@
     hid = hid2 // 2
     ch = hid // NCH
     span = n_col * t
-    wu = decode(up_codes, up_scales)
-    wd = decode(down_codes, down_scales)
     x = activations.reshape(nz, t, feats)
     dy = out_grad.reshape(nz, t, feats)
     hbm = pl.BlockSpec(memory_space=pl.ANY)
     vmem = pl.BlockSpec(memory_space=pltpu.VMEM)
     dma = pltpu.SemaphoreType.DMA
-    return pl.pallas_call(
+    out, in_grad, up_grad, down_grad = pl.pallas_call(
         functools.partial(kernel, nz),
         out_shape=(
             jax.ShapeDtypeStruct((tok, feats), BF16),
             jax.ShapeDtypeStruct((tok, feats), BF16),
             jax.ShapeDtypeStruct((feats, hid2), BF16),
-            jax.ShapeDtypeStruct((hid2, feats), BF16),
+            jax.ShapeDtypeStruct((feats, hid2), BF16),
         ),
-        in_specs=[hbm] * 4,
+        in_specs=[hbm] * 4 + [vmem] * 2,
         out_specs=(vmem, vmem, hbm, hbm),
         scratch_shapes=[
             pltpu.VMEM((2, 2, nz, span, feats), BF16),
             pltpu.VMEM((NCH, 2, feats, ch), BF16),
-            pltpu.VMEM((NCH, 2, ch, feats), BF16),
+            pltpu.VMEM((NCH, 2, feats, ch), BF16),
             pltpu.VMEM((2, NCH, nz, span, ch), BF16),
             pltpu.VMEM((2, NCH, nz - 1, span, ch), BF16),
             pltpu.VMEM((2, span, ch), F32),
             pltpu.VMEM((2, NCH, nz, span, ch), BF16),
             pltpu.VMEM((NCH, 2, feats, ch), F32),
-            pltpu.VMEM((NCH, 2, ch, feats), F32),
+            pltpu.VMEM((NCH, 2, feats, ch), F32),
             pltpu.VMEM((2, 2, span, feats), F32),
             pltpu.VMEM((2, nz, 16, t, feats), BF16),
             pltpu.VMEM((2, nz, 15, t, feats), BF16),
             pltpu.VMEM((NCH, 2, feats // 2, ch), BF16),
-            pltpu.VMEM((NCH, 2, ch // 2, feats), BF16),
             pltpu.VMEM((NCH, 2, feats // 2, ch), BF16),
-            pltpu.VMEM((NCH, 2, ch // 2, feats), BF16),
+            pltpu.VMEM((NCH, 2, feats // 2, ch), BF16),
+            pltpu.VMEM((NCH, 2, feats // 2, ch), BF16),
             pltpu.VMEM((NCH, feats // 2, ch), BF16),
-            pltpu.VMEM((NCH, ch // 2, feats), BF16),
+            pltpu.VMEM((NCH, feats // 2, ch), BF16),
+            pltpu.VMEM((2, NCH, feats, ch), jnp.int32),
+            pltpu.VMEM((2, NCH, feats // 2, ch), jnp.int32),
+            pltpu.VMEM((2, NCH, feats // 2, ch), BF16),
+            pltpu.VMEM((feats, ch), F32),
             dma((3, NCH)),
+            dma((2, 2, NCH)),
             dma((2, 16)),
             dma((2, 16)),
             dma((2, 2, NCH)),
@@ -463,7 +512,8 @@
             collective_id=0, has_side_effects=True, vmem_limit_bytes=62 * 1024 * 1024
         ),
         name="ffn_ring",
-    )(x, dy, wu, wd)
+    )(x, dy, up_codes, down_codes.T, up_scales, down_scales)
+    return out, in_grad, up_grad, down_grad.T
 
 
 def solution(mesh):

time: 203 us -> 186 us (0.916)
  other arithmetic: 8.93 us -> 0 us
  Pallas kernels: 178 us -> 174 us
  local copies, waits for them, and re-layouts: 14.5 us -> 11.1 us
    convert_element_type x2 -> x0, other arithmetic: 8.88 us -> none  [decode(): return jnp.where(negative, -value, value).astype(BF16).reshape(rows, cols)]
    pallas_call x3 -> x0, local copies, waits for them, and re-layouts: 5.82 us -> none  [body(): pl.pallas_call(functools.partial(kernel, nz), out_shape=(jax.ShapeDtypeSt...]
    pallas_call x1, Pallas kernels: 178 us -> 174 us  [body(): pl.pallas_call(functools.partial(kernel, nz), out_shape=(jax.ShapeDtypeSt...]
    unnamed x20 -> x8, local copies, waits for them, and re-layouts: 8.72 us -> 11.1 us
where the time goes in v2:
time: 186 us
  Pallas kernels  174 us (94%)
  local copies, waits for them, and re-layouts  11.1 us (6%)
    pallas_call x1, Pallas kernels, body(): pl.pallas_call(functools.partial(kernel, nz), out_shape=(jax.ShapeDtypeSt...  174 us
    unnamed x8, local copies, waits for them, and re-layouts  11.1 us

profile of v2, /device:TPU:1, one launch (start us, length us, event | category | flops | bytes accessed | tf_op | source)
XLA Modules:
  0.0 185.7 jit_solution(12132724136038767393)
XLA Ops:
  0.6 1.7 copy.10
  2.3 1.7 copy.11
  3.9 173.9 %ffn_ring.1 = (bf16[128,448]{1,0:T(8,128)(2,1)}, bf16[128,448]{1,0:T(8,128)(2,1)}, bf16[448,2304]{1,0:T(8,128)(2,1)}, bf16[448,2304]{1,0:T(8,128)(2,1)}) custom-call(bf16[8,16,448]{2,1,0:T(8,128)(2,1)} %bitcast.6, bf16[8,16,448]{2,1,0:T(8,128)(2,1)} %bitcast.7, s32[448,2304]{1,0:T(8,128)} %cu_in.1, s32[448,2304]{1,0:T(8,128)} %bitcast.4, s32[14,2304]{1,0:T(8,128)} %su_in.1, ...), custom_call_target="tpu_custom_call" | custom-call | tf_op jit(solution)/shard_map/ffn_ring/pallas_call | solution.py:462
  177.9 1.7 copy.12
  179.5 1.7 copy.13
  181.2 0.0 copy-start
  181.2 3.2 %copy.16 = bf16[448,2304]{1,0:T(8,128)(2,1)} copy(bf16[448,2304]{1,0:T(8,128)(2,1)} %get-tuple-element.22) | data formatting | bytes 4128768
  184.4 0.0 copy-done
  184.4 1.3 copy.17
Async XLA Ops:
  181.2 3.2 %copy-start = (bf16[448,2304]{1,0:T(8,128)(2,1)S(1)}, bf16[448,2304]{1,0:T(8,128)(2,1)}, u32[]{:S(2)}) copy-start(bf16[448,2304]{1,0:T(8,128)(2,1)} %get-tuple-element.11) | copy-start | bytes 6193156

commit v3 on v2

--- a/solution.py
+++ b/solution.py
@@ -10,6 +10,7 @@
 MESH = pl.DeviceIdType.MESH
 BLOCK = 32
 NCH = 3
+LAG = 1
 F32 = jnp.float32
 BF16 = jnp.bfloat16
 GATHER = (("ya", "yb", "xa", "xb"), ("ya", "xb", "xa", "yb"))
@@ -219,13 +220,7 @@
             return nn(tok_v[0, 0, b], wu_v[j, 0]) + nn(tok_v[0, 1, b], wu_v[j, 1])
         return nn(tok_v[1, 0, b], wd_v[j, 0]) + nn(tok_v[1, 1, b], wd_v[j, 1])
 
-    def rs_step(i, carry):
-        s, j = i // NCH, i % NCH
-
-        @pl.when(i == 1)
-        def _():
-            w_relay(2)
-
+    def rs_step(s, j):
         @pl.when(s == 0)
         def _():
             for m in range(2):
@@ -241,9 +236,6 @@
 
             rs_snd[m, j, s] = (part + rs_rcv[m, j, s].astype(F32)).astype(BF16)
             rs_copy(m, j, s).start()
-        return carry
-
-    lax.fori_loop(0, NCH * (nz - 1), rs_step, 0)
 
     def ag_copy(m, j, s):
         return remote(ag.at[m, j, s], ag.at[m, j, s + 1], ag_ss.at[m, j, s], ag_rs.at[m, j, s + 1], ring[m])
@@ -252,7 +244,7 @@
         here = ag.at[m, j, s]
         remote(here, here, ag_ss.at[m, j, s], ag_rs.at[m, j, s], twin).wait_recv()
 
-    def gelu_step(j, carry):
+    def gelu_step(j):
         for m in range(2):
             pre_v[m] = term(m, j, z)
         for m in range(2):
@@ -265,10 +257,8 @@
         ag[1, j, 0] = (back * (cdf + pre * density)).astype(BF16)
         for m in range(2):
             ag_copy(m, j, 0).start()
-        return carry
-
-    lax.fori_loop(0, NCH, gelu_step, 0)
-
+
+    slots = acc.shape[0]
     widths = (8, 4, 2, 1)
     offs = (0, 8, 12, 14)
 
@@ -283,7 +273,7 @@
         for code in range(16):
             dims = tuple(HALVE[m][k] for k in range(4) if code >> (3 - k) & 1)
             nyl, ncol = place(dims)
-            obuf[m, s, code] = acc[m, nyl, rows(ncol * t, t)].astype(BF16)
+            obuf[m, s, code] = acc[s % slots, m, nyl, rows(ncol * t, t)].astype(BF16)
         p_copy(m, 0, s).start()
 
     def p_next(m, k, s):
@@ -306,8 +296,7 @@
                 for m in range(2):
                     p_next(m, k, q)
 
-    def ag_step(i, carry):
-        s, j = i // NCH, i % NCH
+    def ag_step(s, j):
         for m in range(2):
 
             @pl.when(s > 0)
@@ -320,11 +309,11 @@
 
         @pl.when(j == 0)
         def _():
-            acc[...] = jnp.zeros_like(acc)
+            acc[s % slots] = jnp.zeros(acc.shape[1:], F32)
 
         for y in range(2):
-            acc[0, y] += nt(ag[0, j, s], wd_v[j, y])
-            acc[1, y] += nt(ag[1, j, s], wu_v[j, y])
+            acc[s % slots, 0, y] += nt(ag[0, j, s], wd_v[j, y])
+            acc[s % slots, 1, y] += nt(ag[1, j, s], wu_v[j, y])
 
         @pl.when(s % 2 == 1)
         def _():
@@ -336,16 +325,6 @@
                 dg[j, y] += tn(jnp.concatenate([tok_v[1, y, a0], tok_v[1, y, a1]], axis=0), a_pair)
                 ug[j, y] += tn(jnp.concatenate([tok_v[0, y, h0], tok_v[0, y, h1]], axis=0), h_pair)
 
-        @pl.when(j == NCH - 1)
-        def _():
-            for m in range(2):
-                p_first(m, s)
-            p_step(s)
-
-        return carry
-
-    lax.fori_loop(0, NCH * nz, ag_step, 0)
-
     def t_pair(m, j):
         src, dst = ((gs_u, gr_u), (gs_d, gr_d))[m]
         return remote(src.at[j], dst.at[j], t_snd.at[0, m, j], t_rcv.at[0, m, j], twin)
@@ -374,17 +353,13 @@
     def t_relay(m, j, who):
         return remote(near[m].at[j], home(m, j, oh, who), t_snd.at[3, m, j], t_rcv.at[3, m, j], twin)
 
-    def t_a(j, carry):
+    def t_a(j):
         for m in range(2):
             for y in range(2):
                 (gs_u, gs_d)[m][j, y] = grad_half(m, j, y, orep).astype(BF16)
             t_pair(m, j).start()
-        return carry
-
-    lax.fori_loop(0, NCH, t_a, 0)
-    p_step(nz)
-
-    def t_b(j, carry):
+
+    def t_b(j):
         for m in range(2):
             t_pair(m, j).wait_recv()
             for y in range(2):
@@ -392,20 +367,58 @@
             t_near(m, j).start()
             t_own(m, j).start()
             t_twin(m, j, rep).start()
-        return carry
-
-    lax.fori_loop(0, NCH, t_b, 0)
-    for s in range(nz + 1, nz + 4):
-        p_step(s)
-
-    def t_c(j, carry):
+
+    def t_c(j):
         for m in range(2):
             t_near(m, j).wait_recv()
             t_far(m, j).start()
             t_relay(m, j, rep).start()
+
+    def ring_step(i, carry):
+        j = i % NCH
+        q = i // NCH - LAG * j
+        s = q - (nz - 1)
+
+        @pl.when(i == 2 * NCH - 1)
+        def _():
+            w_relay(2)
+
+        @pl.when(jnp.logical_and(q >= 0, q < nz - 1))
+        def _():
+            rs_step(q, j)
+
+        @pl.when(q == nz - 1)
+        def _():
+            gelu_step(j)
+
+        @pl.when(jnp.logical_and(s >= 0, s < nz))
+        def _():
+            ag_step(s, j)
+
+        @pl.when(s == nz - 1)
+        def _():
+            t_a(j)
+
+        @pl.when(s == nz)
+        def _():
+            t_b(j)
+
+        @pl.when(s == nz + 2)
+        def _():
+            t_c(j)
+
+        @pl.when(jnp.logical_and(j == NCH - 1, s >= 0))
+        def _():
+            @pl.when(s < nz)
+            def _():
+                for m in range(2):
+                    p_first(m, s)
+
+            p_step(s)
+
         return carry
 
-    lax.fori_loop(0, NCH, t_c, 0)
+    lax.fori_loop(0, NCH * (2 * nz + 3 + LAG * (NCH - 1)), ring_step, 0)
 
     def drain_t(j, carry):
         for m in range(2):
@@ -479,7 +492,7 @@
             pltpu.VMEM((2, NCH, nz, span, ch), BF16),
             pltpu.VMEM((NCH, 2, feats, ch), F32),
             pltpu.VMEM((NCH, 2, feats, ch), F32),
-            pltpu.VMEM((2, 2, span, feats), F32),
+            pltpu.VMEM((LAG * (NCH - 1) + 1, 2, 2, span, feats), F32),
             pltpu.VMEM((2, nz, 16, t, feats), BF16),
             pltpu.VMEM((2, nz, 15, t, feats), BF16),
             pltpu.VMEM((NCH, 2, feats // 2, ch), BF16),

time: 186 us -> 181 us (0.973); the launches traced: 186 us -> 178 us
  Pallas kernels: 174 us -> 166 us
    pallas_call x1, Pallas kernels: 174 us -> 166 us  [body(): pl.pallas_call(functools.partial(kernel, nz), out_shape=(jax.ShapeDtypeSt...]
where the time goes in v3:
time: 181 us; the launch traced here: 178 us
  Pallas kernels  166 us (92%)
  local copies, waits for them, and re-layouts  11.1 us (6%)
    pallas_call x1, Pallas kernels, body(): pl.pallas_call(functools.partial(kernel, nz), out_shape=(jax.ShapeDtypeSt...  166 us
    unnamed x8, local copies, waits for them, and re-layouts  11.1 us

profile of v3, /device:TPU:1, one launch (start us, length us, event | category | flops | bytes accessed | tf_op | source)
XLA Modules:
  0.0 177.7 jit_solution(11945085022611068272)
XLA Ops:
  0.6 1.7 copy.10
  2.3 1.7 copy.11
  3.9 165.9 %ffn_ring.1 = (bf16[128,448]{1,0:T(8,128)(2,1)}, bf16[128,448]{1,0:T(8,128)(2,1)}, bf16[448,2304]{1,0:T(8,128)(2,1)}, bf16[448,2304]{1,0:T(8,128)(2,1)}) custom-call(bf16[8,16,448]{2,1,0:T(8,128)(2,1)} %bitcast.6, bf16[8,16,448]{2,1,0:T(8,128)(2,1)} %bitcast.7, s32[448,2304]{1,0:T(8,128)} %cu_in.1, s32[448,2304]{1,0:T(8,128)} %bitcast.4, s32[14,2304]{1,0:T(8,128)} %su_in.1, ...), custom_call_target="tpu_custom_call" | custom-call | tf_op jit(solution)/shard_map/ffn_ring/pallas_call | solution.py:475
  169.9 1.7 copy.12
  171.5 1.7 copy.13
  173.2 0.0 copy-start
  173.2 3.2 %copy.16 = bf16[448,2304]{1,0:T(8,128)(2,1)} copy(bf16[448,2304]{1,0:T(8,128)(2,1)} %get-tuple-element.22) | data formatting | bytes 4128768
  176.4 0.0 copy-done
  176.4 1.3 copy.17
Async XLA Ops:
  173.2 3.2 %copy-start = (bf16[448,2304]{1,0:T(8,128)(2,1)S(1)}, bf16[448,2304]{1,0:T(8,128)(2,1)}, u32[]{:S(2)}) copy-start(bf16[448,2304]{1,0:T(8,128)(2,1)} %get-tuple-element.11) | copy-start | bytes 6193156

commit v4 on v3

--- a/solution.py
+++ b/solution.py
@@ -97,6 +97,15 @@
             return pltpu.make_async_copy(src.at[rows(rep * fh, fh), lanes(oh, j)], c_far.at[m, j], c_sem.at[1, m, j])
         return pltpu.make_async_copy(src.at[:, lanes(yl, j)], c_own.at[m, j], c_sem.at[0, m, j])
 
+    tok_in = (x_in, dy_in)
+
+    def tok_local(m, k):
+        b = (z + nz - 1 - k) % nz if m == 0 else (z + 1 + k) % nz
+        return pltpu.make_async_copy(tok_in[m].at[b], tok_v.at[m, yl, k, rows(col * t, t)], loc_sem.at[m, k])
+
+    for k in range(nz):
+        for m in range(2):
+            tok_local(m, k).start()
     for far in (True, False):
         for j in range(NCH):
             for m in range(2):
@@ -141,30 +150,33 @@
 
         lax.fori_loop(0, count, step, 0)
 
-    tok_in = (x_in, dy_in)
-
-    def spot(m, code):
+    gz = nz // 2
+
+    def spot(m, code, g):
         dims = tuple(GATHER[m][k] for k in range(4) if code >> k & 1)
         nyl, ncol = place(dims)
-        return tok_v.at[m, nyl, :, rows(ncol * t, t)]
-
-    def g_copy(m, code, step):
-        src = tok_in[m] if code == 0 else spot(m, code)
+        return tok_v.at[m, nyl, pl.ds(g * gz, gz), rows(ncol * t, t)]
+
+    def g_copy(m, code, step, g):
         new = code + 2**step
-        return remote(src, spot(m, code), g_snd.at[m, new], g_rcv.at[m, new], plane(GATHER[m][step]))
-
-    def g_wait(m, code):
-        here = spot(m, code)
-        remote(here, here, g_snd.at[m, code], g_rcv.at[m, code], twin).wait_recv()
-
-    for step in range(1, 4):
-        for m in range(2):
-            g_copy(m, 0, step).start()
-    for m in range(2):
-        g_copy(m, 0, 0).start()
-    tok_local = [pltpu.make_async_copy(tok_in[m], spot(m, 0), loc_sem.at[2, m]) for m in range(2)]
-    for m in range(2):
-        tok_local[m].start()
+        here = spot(m, code, g)
+        return remote(here, here, g_snd.at[m, new, g], g_rcv.at[m, new, g], plane(GATHER[m][step]))
+
+    def g_pass(code, g):
+        for m in range(2):
+            here = spot(m, code, g)
+            remote(here, here, g_snd.at[m, code, g], g_rcv.at[m, code, g], twin).wait_recv()
+            for step in range(4):
+                if 2**step > code:
+                    g_copy(m, code, step, g).start()
+
+    for g in range(2):
+        for k in range(g * gz, g * gz + gz):
+            for m in range(2):
+                tok_local(m, k).wait()
+        for step in (3, 2, 1, 0) if g == 0 else (0,):
+            for m in range(2):
+                g_copy(m, 0, step, g).start()
 
     def w_send(j):
         for m in range(2):
@@ -190,23 +202,20 @@
         5: lambda: w_decode(1, 0, False),
         6: lambda: w_decode(0, 1, False),
         7: lambda: w_decode(1, 1, False),
-        8: lambda: w_decode(0, 2, False),
-        9: lambda: w_decode(1, 2, False),
-        10: clear,
-        12: lambda: w_relay(0),
-        14: lambda: w_relay(1),
+        9: lambda: w_decode(0, 2, False),
+        10: lambda: w_decode(1, 2, False),
+        11: clear,
+        13: lambda: w_relay(0),
     }
     w_send(0)
     for code in range(1, 16):
         if code in between:
             between[code]()
-        for m in range(2):
-            g_wait(m, code)
-            for step in range(4):
-                if 2**step > code:
-                    g_copy(m, code, step).start()
-    for m in range(2):
-        tok_local[m].wait()
+        g_pass(code, 0)
+        if code == 7:
+            for step in (3, 2, 1):
+                for m in range(2):
+                    g_copy(m, 0, step, 1).start()
 
     def rs_copy(m, j, s):
         return remote(rs_snd.at[m, j, s], rs_rcv.at[m, j, s + 1], rs_ss.at[m, j, s], rs_rs.at[m, j, s + 1], ring[m])
@@ -227,8 +236,7 @@
                 w_second(m, j).wait_recv()
 
         for m in range(2):
-            b = (z + nz - 1 - s) % nz if m == 0 else (z + 1 + s) % nz
-            part = term(m, j, b)
+            part = term(m, j, s)
 
             @pl.when(s > 0)
             def _():
@@ -246,7 +254,7 @@
 
     def gelu_step(j):
         for m in range(2):
-            pre_v[m] = term(m, j, z)
+            pre_v[m] = term(m, j, nz - 1)
         for m in range(2):
             rs_wait(m, j, nz - 1)
         pre = pre_v[0] + rs_rcv[0, j, nz - 1].astype(F32)
@@ -319,11 +327,10 @@
         def _():
             a_pair = jnp.concatenate([ag[0, j, s - 1], ag[0, j, s]], axis=0)
             h_pair = jnp.concatenate([ag[1, j, s - 1], ag[1, j, s]], axis=0)
-            a0, a1 = (z + nz - s + 1) % nz, (z + nz - s) % nz
-            h0, h1 = (z + s - 1) % nz, (z + s) % nz
+            k0, k1 = nz - s, nz - 1 - s
             for y in range(2):
-                dg[j, y] += tn(jnp.concatenate([tok_v[1, y, a0], tok_v[1, y, a1]], axis=0), a_pair)
-                ug[j, y] += tn(jnp.concatenate([tok_v[0, y, h0], tok_v[0, y, h1]], axis=0), h_pair)
+                dg[j, y] += tn(jnp.concatenate([tok_v[1, y, k0], tok_v[1, y, k1]], axis=0), a_pair)
+                ug[j, y] += tn(jnp.concatenate([tok_v[0, y, k0], tok_v[0, y, k1]], axis=0), h_pair)
 
     def t_pair(m, j):
         src, dst = ((gs_u, gr_u), (gs_d, gr_d))[m]
@@ -379,9 +386,19 @@
         q = i // NCH - LAG * j
         s = q - (nz - 1)
 
-        @pl.when(i == 2 * NCH - 1)
-        def _():
-            w_relay(2)
+        last = gz * NCH - 1
+        for k in range(last + 1):
+
+            @pl.when(i == k)
+            def _():
+                for code in (k + 1,) if k < last else range(k + 1, 16):
+                    g_pass(code, 1)
+
+        for k in range(1, NCH):
+
+            @pl.when(i == k * NCH - 1)
+            def _():
+                w_relay(k)
 
         @pl.when(jnp.logical_and(q >= 0, q < nz - 1))
         def _():
@@ -456,7 +473,8 @@
         for code in range(8):
             for step in range(4):
                 if 2**step > code:
-                    g_copy(m, code, step).wait_send()
+                    for g in range(2):
+                        g_copy(m, code, step, g).wait_send()
 
 
 def body(n_row, n_col, activations, out_grad, up_codes, up_scales, down_codes, down_scales):
@@ -505,10 +523,10 @@
             pltpu.VMEM((2, NCH, feats // 2, ch), jnp.int32),
             pltpu.VMEM((2, NCH, feats // 2, ch), BF16),
             pltpu.VMEM((feats, ch), F32),
-            dma((3, NCH)),
+            dma((2, nz)),
             dma((2, 2, NCH)),
-            dma((2, 16)),
-            dma((2, 16)),
+            dma((2, 16, 2)),
+            dma((2, 16, 2)),
             dma((2, 2, NCH)),
             dma((2, 2, NCH)),
             dma((2, NCH, nz)),

time: 181 us -> 175 us (0.967)
  Pallas kernels: 166 us -> 160 us
    pallas_call x1, Pallas kernels: 166 us -> 160 us  [body(): pl.pallas_call(functools.partial(kernel, nz), out_shape=(jax.ShapeDtypeSt...]
where the time goes in v4:
time: 175 us; the launch traced here: 172 us
  Pallas kernels  160 us (91%)
  local copies, waits for them, and re-layouts  11.1 us (6%)
    pallas_call x1, Pallas kernels, body(): pl.pallas_call(functools.partial(kernel, nz), out_shape=(jax.ShapeDtypeSt...  160 us
    unnamed x8, local copies, waits for them, and re-layouts  11.1 us

profile of v4, /device:TPU:1, one launch (start us, length us, event | category | flops | bytes accessed | tf_op | source)
XLA Modules:
  0.0 172.1 jit_solution(15162559962405654743)
XLA Ops:
  0.6 1.7 copy.10
  2.3 1.7 copy.11
  3.9 160.3 %ffn_ring.1 = (bf16[128,448]{1,0:T(8,128)(2,1)}, bf16[128,448]{1,0:T(8,128)(2,1)}, bf16[448,2304]{1,0:T(8,128)(2,1)}, bf16[448,2304]{1,0:T(8,128)(2,1)}) custom-call(bf16[8,16,448]{2,1,0:T(8,128)(2,1)} %bitcast.6, bf16[8,16,448]{2,1,0:T(8,128)(2,1)} %bitcast.7, s32[448,2304]{1,0:T(8,128)} %cu_in.1, s32[448,2304]{1,0:T(8,128)} %bitcast.4, s32[14,2304]{1,0:T(8,128)} %su_in.1, ...), custom_call_target="tpu_custom_call" | custom-call | tf_op jit(solution)/shard_map/ffn_ring/pallas_call | solution.py:493
  164.3 1.7 copy.12
  166.0 1.7 copy.13
  167.6 0.0 copy-start
  167.6 3.2 %copy.16 = bf16[448,2304]{1,0:T(8,128)(2,1)} copy(bf16[448,2304]{1,0:T(8,128)(2,1)} %get-tuple-element.22) | data formatting | bytes 4128768
  170.8 0.0 copy-done
  170.8 1.3 copy.17
Async XLA Ops:
  167.6 3.2 %copy-start = (bf16[448,2304]{1,0:T(8,128)(2,1)S(1)}, bf16[448,2304]{1,0:T(8,128)(2,1)}, u32[]{:S(2)}) copy-start(bf16[448,2304]{1,0:T(8,128)(2,1)} %get-tuple-element.11) | copy-start | bytes 6193156
